TPU v7x, 256 devices: a whole 4x4x8 slice. The times are simulated.
256 devices in a mesh: blk: 64 (over x, z, y_lo), uly: 4 (over y_hi, core).
Axes of the slice: x: 4, y: 4 (y_hi: 2, y_lo: 2; y = y_hi * 2 + y_lo), z: 8, core: 2. Of those that a mesh axis runs over, the one named last changes fastest.
Arguments:
- tokens: bfloat16 [6144, 2560], P(('blk', 'uly')), may hold values from -6 to 6
- in_bits: int32 [6144, 2560], P(('blk', 'uly')), may hold values from 0 to 1
- qkv_weights: bfloat16 [2, 3, 2560, 2560], P(None, None, 'blk', 'uly'), may hold values from -0.125 to 0.125
- qkv_bits: int32 [6144, 3, 2560], P('blk', None, 'uly'), may hold values from 0 to 1
- gain_query: float32 [2560], P('uly'), may hold values from 0.7 to 1.8
- gain_key: float32 [2560], P('uly'), may hold values from 0.7 to 1.8
- out_weights: bfloat16 [2, 2560, 2560], P(None, 'uly', 'blk'), may hold values from -0.5 to 0.5
- mix_bits: int32 [6144, 2560], P('blk', 'uly'), may hold values from 0 to 1
- out_bits: int32 [6144, 2560], P('blk'), may hold values from 0 to 1
Outputs:
- layer_output: bfloat16 [6144, 2560], P(('blk', 'uly'))
Inputs may be any that keep to these rules, and one draw needn't show every extreme that they name: `in_bits`: a bit of 1 stands for the sign +1, a bit of 0 for -1. `qkv_bits`: a bit of 1 stands for the sign +1, a bit of 0 for -1. `mix_bits`: a bit of 1 stands for the sign +1, a bit of 0 for -1. `out_bits`: a bit of 1 stands for the sign +1, a bit of 0 for -1.
All inputs are finite; a program needn't handle non-finite values.
Results may differ from a plain program's by a relative error of at most 0.018.
Values may be sent and summed in bfloat16 or wider, within the bound.
A program may use at most 128 MiB of HBM per device.

v0:
```python
import math
import jax
import jax.numpy as jnp
from jax import lax
from jax.sharding import PartitionSpec as P

HEAD = 128
epsilon = 1e-06


def signed(bit_values):
    return (2 * bit_values - 1).astype(jnp.float32)


def normalize(values, gain_vector):
    row_count = values.shape[0]
    by_head = values.astype(jnp.float32).reshape(row_count, -1, HEAD)
    inverse_rms = lax.rsqrt(jnp.mean(by_head * by_head, axis=-1, keepdims=True) + epsilon)
    return (by_head * inverse_rms * gain_vector.reshape(-1, HEAD)).astype(jnp.bfloat16)


def body(
    tokens, in_bits, qkv_weights, qkv_bits, gain_query, gain_key, out_weights, mix_bits, out_bits
):
    flipped = (tokens.astype(jnp.float32) * signed(in_bits)).astype(jnp.bfloat16)
    group_rows = lax.all_gather(jnp.stack([tokens, flipped]), "uly", axis=1, tiled=True)
    row_total = group_rows.shape[1]
    projections = jnp.einsum(
        "mrd,mkdc->rmkc",
        group_rows,
        lax.all_gather(qkv_weights, "blk", axis=2, tiled=True),
        preferred_element_type=jnp.float32,
    )
    projected = (projections[:, 0] + signed(qkv_bits) * projections[:, 1]).astype(jnp.bfloat16)
    queries = normalize(projected[:, 0], gain_query)
    head_count = queries.shape[1]
    keys_normed = normalize(projected[:, 1], gain_key).reshape(row_total, -1)
    values_block = projected[:, 2]
    score_scale = 1.0 / math.sqrt(HEAD)

    def attend(running, shard_piece):
        numerator, denominator = running
        key_rows = shard_piece[0].reshape(shard_piece[0].shape[0], head_count, HEAD)
        value_rows = shard_piece[1].reshape(shard_piece[1].shape[0], head_count, HEAD)
        scores = (
            jnp.einsum("rhd,nhd->hrn", queries, key_rows, preferred_element_type=jnp.float32)
            * score_scale
        )
        weights = jnp.exp(scores).astype(jnp.bfloat16)
        numerator = numerator + jnp.einsum(
            "hrn,nhd->rhd", weights, value_rows, preferred_element_type=jnp.float32
        )
        denominator = denominator + jnp.sum(weights.astype(jnp.float32), axis=2).T
        return (numerator, denominator)

    start_state = (
        jnp.zeros((row_total, head_count, HEAD), jnp.float32),
        jnp.zeros((row_total, head_count), jnp.float32),
    )
    all_keys, all_values = (
        lax.all_gather(keys_normed, "blk", axis=0, tiled=True),
        lax.all_gather(values_block, "blk", axis=0, tiled=True),
    )
    group_count = lax.axis_size("blk")
    per_block = 1
    while per_block * row_total < 512 and group_count % (per_block * 2) == 0:
        per_block = per_block * 2
    block_rows = per_block * row_total
    block_count = group_count // per_block
    key_blocks = all_keys.reshape(block_count, block_rows, all_keys.shape[1])
    value_blocks = all_values.reshape(block_count, block_rows, all_values.shape[1])

    def scan_step(running, block_pair):
        return (attend(running, block_pair), None)

    (numerator, denominator), unused = lax.scan(scan_step, start_state, (key_blocks, value_blocks))
    attended = (numerator / denominator[:, :, None]).astype(jnp.bfloat16).reshape(row_total, -1)
    attended_flipped = (attended.astype(jnp.float32) * signed(mix_bits)).astype(jnp.bfloat16)
    attended_pair = jnp.stack([attended, attended_flipped])
    out_signs = signed(out_bits)
    partial_out = jnp.einsum(
        "mrc,mcn->rmn",
        attended_pair,
        lax.all_gather(out_weights, "blk", axis=2, tiled=True),
        preferred_element_type=jnp.float32,
    )
    summed = lax.psum_scatter(
        partial_out.astype(jnp.bfloat16), "uly", scatter_dimension=0, tiled=True
    ).astype(jnp.float32)
    own_rows = summed.shape[0]
    own_signs = lax.dynamic_slice_in_dim(out_signs, lax.axis_index("uly") * own_rows, own_rows, 0)
    result_rows = summed[:, 0] + own_signs * summed[:, 1]
    return result_rows.astype(jnp.bfloat16)


def solution(mesh):
    return jax.shard_map(
        body,
        mesh=mesh,
        in_specs=(
            P(("blk", "uly"), None),
            P(("blk", "uly"), None),
            P(None, None, "blk", "uly"),
            P("blk", None, "uly"),
            P("uly"),
            P("uly"),
            P(None, "uly", "blk"),
            P("blk", "uly"),
            P("blk", None),
        ),
        out_specs=P(("blk", "uly"), None),
        check_vma=False,
    )
```

profile of v0, /device:TPU:1, one launch (start us, length us, event | category | flops | bytes accessed | tf_op | source)
XLA Modules:
  0.0 1435.4 jit_solution(2879353111804736999)
XLA Ops:
  6.5 0.7 all-gather.6.cloned.1.call-update
  7.3 1.1 fusion.17
  8.4 0.9 pad_maximum_fusion
  9.3 12.7 all_gather.15
  22.0 423.9 %all-gather.6.cloned.1.call-done = bf16[2,3,2560,640]{3,2,1,0:T(8,128)(2,1)} async-done(((bf16[2,3,40,640]{3,2,1,0:T(8,128)(2,1)}), bf16[2,3,2560,640]{3,2,1,0:T(8,128)(2,1)}) %all-gather.6.cloned.1.call-update) | async-done | bytes 19660816 | tf_op jit(solution)/shard_map/all_gather | solution.py:31
  445.9 8.3 convolution_bitcast_fusion.1
  454.2 0.2 fusion.5
  454.4 0.2 copy.28
  454.8 0.7 fusion.8
  455.6 0.7 slice_convert_fusion
  456.4 0.5 all-gather.10.cloned.1.call-update
  457.0 0.2 copy.30
  457.5 268.4 %all-gather.8.cloned.1.call-done = bf16[6144,640]{1,0:T(8,128)(2,1)} async-done(((bf16[96,640]{1,0:T(8,128)(2,1)}), bf16[6144,640]{1,0:T(8,128)(2,1)}) %all-gather.8.cloned.1.call-update) | async-done | bytes 7864336 | tf_op jit(solution)/shard_map/all_gather | solution.py:61
  726.0 311.0 %all-gather.12.cloned.1.call-done = bf16[6144,1,640]{2,0,1:T(8,128)(2,1)} async-done(((bf16[96,1,640]{2,0,1:T(8,128)(2,1)}), bf16[6144,1,640]{2,0,1:T(8,128)(2,1)}) %all-gather.12.cloned.1.call-update) | async-done | bytes 7864336 | tf_op jit(solution)/shard_map/all_gather | solution.py:62
  1037.0 31.7 %while.13 = (s32[]{:T(128)}, f32[96,5,128]{2,0,1:T(8,128)S(1)}, f32[96,5]{0,1:T(8,128)S(1)}, bf16[8,768,640]{2,1,0:T(8,128)(2,1)}, bf16[8,768,640]{2,1,0:T(8,128...) while((s32[]{:T(128)}, f32[96,5,128]{2,0,1:T(8,128)S(1)}, ...), condition=%wide.region_4.5_spmd.clone, body=%wide.region_2.4_spmd.clone.sunk | while | flops 190341600 | bytes 11927140 | solution.py:76
  1037.0 1.7 constant_dynamic-slice_fusion.3
  1038.7 0.6 copy.51
  1039.3 0.5 convert_reduce_fusion.2
  1039.8 0.6 copy.50
  1040.5 0.5 fusion.35
  1040.9 1.7 constant_dynamic-slice_fusion.3
  1042.6 0.6 copy.51
  1043.3 0.5 convert_reduce_fusion.2
  1043.8 0.6 copy.50
  1044.4 0.5 fusion.35
  1044.9 1.7 constant_dynamic-slice_fusion.3
  1046.6 0.6 copy.51
  1047.3 0.5 convert_reduce_fusion.2
  1047.7 0.6 copy.50
  1048.4 0.5 fusion.35
  1048.9 1.7 constant_dynamic-slice_fusion.3
  1050.6 0.6 copy.51
  1051.2 0.5 convert_reduce_fusion.2
  1051.7 0.6 copy.50
  1052.4 0.5 fusion.35
  1052.9 1.7 constant_dynamic-slice_fusion.3
  1054.5 0.6 copy.51
  1055.2 0.5 convert_reduce_fusion.2
  1055.7 0.6 copy.50
  1056.3 0.5 fusion.35
  1056.8 1.7 constant_dynamic-slice_fusion.3
  1058.5 0.6 copy.51
  1059.2 0.5 convert_reduce_fusion.2
  1059.6 0.6 copy.50
  1060.3 0.5 fusion.35
  1060.8 1.7 constant_dynamic-slice_fusion.3
  1062.5 0.6 copy.51
  1063.1 0.5 convert_reduce_fusion.2
  1063.6 0.6 copy.50
  1064.3 0.5 fusion.35
  1064.8 1.7 constant_dynamic-slice_fusion.3
  1066.4 0.6 copy.51
  1067.1 0.5 convert_reduce_fusion.2
  1067.6 0.6 copy.50
  1068.2 0.5 fusion.35
  1069.0 0.2 copy.34
  1069.2 0.2 copy.36
  1069.5 1.0 fusion.18
  1070.5 274.9 %all-gather.10.cloned.1.call-done = bf16[2,640,2560]{1,2,0:T(8,128)(2,1)} async-done(((bf16[2,640,40]{1,2,0:T(8,128)(2,1)}), bf16[2,640,2560]{1,2,0:T(8,128)(2,1)}) %all-gather.10.cloned.1.call-update) | async-done | bytes 6553616 | tf_op jit(solution)/shard_map/all_gather | solution.py:84
  1345.4 5.0 fusion.1
  1350.3 1.0 copy.46
  1351.4 74.8 %reduce-scatter.4.cloned.1.call-done = bf16[24,5120]{1,0:T(8,128)(2,1)} async-done(((bf16[96,5120]{1,0:T(8,128)(2,1)}), bf16[24,5120]{1,0:T(8,128)(2,1)}) %reduce-scatter.4.cloned.1.call-update) | async-done | bytes 245776
  1426.2 1.0 bitcast_convert_fusion
  1427.2 1.7 fusion.11
  (36 shorter events, 1.3 us)
Async XLA Ops:
  6.5 439.4 %all-gather.6.cloned.1.call-start = ((), (), s32[]{:S(2)}) async-start(), calls=%async_computation.1 | async-start | bytes 19968000 | tf_op jit(solution)/shard_map/all_gather | solution.py:31
  7.3 718.7 %all-gather.8.cloned.1.call-start = ((), (), s32[]{:S(2)}) async-start(), calls=%async_computation.2 | async-start | bytes 7987200 | tf_op jit(solution)/shard_map/all_gather | solution.py:61
  22.0 432.2 %copy-start = (s32[96,3,640]{2,0,1:T(8,128)S(1)}, s32[96,3,640]{2,0,1:T(8,128)}, u32[]{:S(2)}) copy-start(s32[96,3,640]{2,0,1:T(8,128)} %param.14) | copy-start | bytes 2211844
  22.0 432.8 %copy-start.1 = (f32[640]{0:T(1024)S(1)}, f32[640]{0:T(1024)}, u32[]{:S(2)}) copy-start(f32[640]{0:T(1024)} %param.16) | copy-start | bytes 7684
  454.2 3.0 copy-start.2
  455.6 581.4 %all-gather.12.cloned.1.call-start = ((), (), s32[]{:S(2)}) async-start(), calls=%async_computation.4 | async-start | bytes 7987200 | tf_op jit(solution)/shard_map/all_gather | solution.py:62
  456.3 889.0 %all-gather.10.cloned.1.call-start = ((), (), s32[]{:S(2)}) async-start(), calls=%async_computation.3 | async-start | bytes 6656000 | tf_op jit(solution)/shard_map/all_gather | solution.py:84
  456.9 969.3 %reduce-scatter.4.cloned.1.call-start = ((), (), s32[]{:S(2)}) async-start(), calls=%async_computation.5 | async-start | bytes 1228800
Sparse Core Ops, SparseCore 0:
  9.2 436.6 all-gather.5
  455.7 270.2 all-gather.7
  727.7 309.1 all-gather.11
  1038.6 306.6 all-gather.9
  1351.5 74.6 reduce-scatter.3
where the time goes:
time: 1440 us
  waiting for transfers between devices  1350 us (94%)
  local copies, waits for them, and re-layouts  26.1 us (2%)
  matrix products  20.8 us (1%)
    all_gather x1, waiting for transfers between devices, body(): lax.all_gather(qkv_weights, 'blk', axis=2, tiled=True)  424 us
    all_gather x1, waiting for transfers between devices, body(): lax.all_gather(values_block, 'blk', axis=0, tiled=True)  311 us
    all_gather x1, waiting for transfers between devices, body(): lax.all_gather(out_weights, 'blk', axis=2, tiled=True)  275 us
    all_gather x1, waiting for transfers between devices, body(): lax.all_gather(keys_normed, 'blk', axis=0, tiled=True)  268 us
    unnamed x6, waiting for transfers between devices  76.1 us
  transfers between devices with their start and end apart: 5, of which 5 were waited for; matrix products, arithmetic and copies ran while one was open for 3% of the time, Pallas kernels for 0%

commit v1 on v0

--- a/solution.py
+++ b/solution.py
@@ -59,7 +59,15 @@
     )
     all_keys, all_values = (
         lax.all_gather(keys_normed, "blk", axis=0, tiled=True),
-        lax.all_gather(values_block, "blk", axis=0, tiled=True),
+        jnp.concatenate(
+            jax.lax.all_to_all(
+                jnp.stack([values_block for _ in range(jax.lax.axis_size("blk"))], axis=0),
+                axis_name="blk",
+                split_axis=0,
+                concat_axis=0,
+            ),
+            0,
+        ),
     )
     group_count = lax.axis_size("blk")
     per_block = 1

time: 1440 us -> 1200 us (0.83)
  waiting for transfers between devices: 1350 us -> 1100 us
    all_gather x1 -> x0, waiting for transfers between devices: 311 us -> none  [body(): lax.all_gather(values_block, 'blk', axis=0, tiled=True)]
    all_gather x1, waiting for transfers between devices: 268 us -> 345 us  [body(): lax.all_gather(keys_normed, 'blk', axis=0, tiled=True)]
    all_gather x1, waiting for transfers between devices: 275 us -> 258 us  [body(): lax.all_gather(out_weights, 'blk', axis=2, tiled=True)]
    unnamed x6 -> x5, waiting for transfers between devices: 76.1 us -> 77.1 us
  transfers between devices with their start and end apart: 5 -> 5, of which waited for: 5 -> 4; matrix products, arithmetic and copies ran while one was open for 3% -> 3% of each run, Pallas kernels for 0% -> 0%
where the time goes in v1:
time: 1200 us
  waiting for transfers between devices  1100 us (92%)
  local copies, waits for them, and re-layouts  29.8 us (2%)
  matrix products  20.8 us (2%)
  between operations  13.3 us (1%)
  blocking collectives  12.7 us (1%)
    all_gather x1, waiting for transfers between devices, body(): lax.all_gather(qkv_weights, 'blk', axis=2, tiled=True)  424 us
    all_gather x1, waiting for transfers between devices, body(): lax.all_gather(keys_normed, 'blk', axis=0, tiled=True)  345 us
    all_gather x1, waiting for transfers between devices, body(): lax.all_gather(out_weights, 'blk', axis=2, tiled=True)  258 us
    unnamed x5, waiting for transfers between devices  77.1 us
  transfers between devices with their start and end apart: 5, of which 4 were waited for; matrix products, arithmetic and copies ran while one was open for 3% of the time, Pallas kernels for 0%

profile of v1, /device:TPU:1, one launch (start us, length us, event | category | flops | bytes accessed | tf_op | source)
XLA Modules:
  0.0 1196.7 jit_solution(16570385090877557660)
XLA Ops:
  6.5 0.7 all-gather.4.cloned.1.call-update
  7.3 1.1 fusion.17
  8.4 0.9 pad_maximum_fusion
  9.3 12.7 %all_gather.12 = bf16[2,96,2560]{2,1,0:T(8,128)(2,1)S(1)} all-gather(bf16[2,24,2560]{2,1,0:T(8,128)(2,1)S(1)} %pad_maximum_fusion), channel_id=1, replica_groups=mesh['blk'=64,'uly'=4] {'uly'}, dimensions={1}, use_global_device_ids=true | all-gather | bytes 1228800 | tf_op jit(solution)/shard_map/all_gather | solution.py:26
  22.0 423.9 %all-gather.4.cloned.1.call-done = bf16[2,3,2560,640]{3,2,1,0:T(8,128)(2,1)} async-done(((bf16[2,3,40,640]{3,2,1,0:T(8,128)(2,1)}), bf16[2,3,2560,640]{3,2,1,0:T(8,128)(2,1)}) %all-gather.4.cloned.1.call-update) | async-done | bytes 19660816 | tf_op jit(solution)/shard_map/all_gather | solution.py:31
  445.9 8.3 convolution_bitcast_fusion.1
  454.2 0.2 fusion.5
  454.4 0.2 copy.39
  454.8 0.7 fusion.8
  455.6 3.7 stack.21
  459.3 8.3 all-to-all-start
  467.6 0.7 all-gather.8.cloned.1.call-update
  468.4 0.2 copy.41
  468.9 344.9 %all-gather.6.cloned.1.call-done = bf16[6144,640]{1,0:T(8,128)(2,1)} async-done(((bf16[96,640]{1,0:T(8,128)(2,1)}), bf16[6144,640]{1,0:T(8,128)(2,1)}) %all-gather.6.cloned.1.call-update) | async-done | bytes 7864336 | tf_op jit(solution)/shard_map/all_gather | solution.py:61
  813.9 31.7 %while.13 = (s32[]{:T(128)}, f32[96,5,128]{2,0,1:T(8,128)S(1)}, f32[96,5]{0,1:T(8,128)S(1)}, bf16[8,768,640]{2,1,0:T(8,128)(2,1)}, bf16[8,768,640]{2,1,0:T(8,128...) while((s32[]{:T(128)}, f32[96,5,128]{2,0,1:T(8,128)S(1)}, ...), condition=%wide.region_4.5_spmd.clone, body=%wide.region_2.4_spmd.clone.sunk | while | flops 190341600 | bytes 11927140 | solution.py:84
  813.9 1.7 constant_dynamic-slice_fusion.3
  815.5 0.6 copy.62
  816.2 0.5 convert_reduce_fusion.2
  816.7 0.6 copy.61
  817.3 0.5 fusion.35
  817.8 1.7 constant_dynamic-slice_fusion.3
  819.5 0.6 copy.62
  820.2 0.5 convert_reduce_fusion.2
  820.6 0.6 copy.61
  821.3 0.5 fusion.35
  821.8 1.7 constant_dynamic-slice_fusion.3
  823.5 0.6 copy.62
  824.1 0.5 convert_reduce_fusion.2
  824.6 0.6 copy.61
  825.3 0.5 fusion.35
  825.8 1.7 constant_dynamic-slice_fusion.3
  827.4 0.6 copy.62
  828.1 0.5 convert_reduce_fusion.2
  828.6 0.6 copy.61
  829.2 0.5 fusion.35
  829.7 1.7 constant_dynamic-slice_fusion.3
  831.4 0.6 copy.62
  832.1 0.5 convert_reduce_fusion.2
  832.5 0.6 copy.61
  833.2 0.5 fusion.35
  833.7 1.7 constant_dynamic-slice_fusion.3
  835.4 0.6 copy.62
  836.0 0.5 convert_reduce_fusion.2
  836.5 0.6 copy.61
  837.2 0.5 fusion.35
  837.7 1.7 constant_dynamic-slice_fusion.3
  839.3 0.6 copy.62
  840.0 0.5 convert_reduce_fusion.2
  840.5 0.6 copy.61
  841.1 0.5 fusion.35
  841.6 1.7 constant_dynamic-slice_fusion.3
  843.3 0.6 copy.62
  844.0 0.5 convert_reduce_fusion.2
  844.5 0.6 copy.61
  845.1 0.5 fusion.35
  845.9 0.2 copy.45
  846.1 0.2 copy.47
  846.4 1.0 fusion.18
  847.4 258.4 %all-gather.8.cloned.1.call-done = bf16[2,640,2560]{1,2,0:T(8,128)(2,1)} async-done(((bf16[2,640,40]{1,2,0:T(8,128)(2,1)}), bf16[2,640,2560]{1,2,0:T(8,128)(2,1)}) %all-gather.8.cloned.1.call-update) | async-done | bytes 6553616 | tf_op jit(solution)/shard_map/all_gather | solution.py:92
  1105.8 5.0 fusion.1
  1110.8 1.0 copy.57
  1111.9 75.7 %reduce-scatter.4.cloned.1.call-done = bf16[24,5120]{1,0:T(8,128)(2,1)} async-done(((bf16[96,5120]{1,0:T(8,128)(2,1)}), bf16[24,5120]{1,0:T(8,128)(2,1)}) %reduce-scatter.4.cloned.1.call-update) | async-done | bytes 245776
  1187.6 1.0 bitcast_convert_fusion
  1188.5 1.7 fusion.11
  (36 shorter events, 1.3 us)
Async XLA Ops:
  6.5 439.4 %all-gather.4.cloned.1.call-start = ((), (), s32[]{:S(2)}) async-start(), calls=%async_computation.2 | async-start | bytes 19968000 | tf_op jit(solution)/shard_map/all_gather | solution.py:31
  7.3 806.6 %all-gather.6.cloned.1.call-start = ((), (), s32[]{:S(2)}) async-start(), calls=%async_computation.3 | async-start | bytes 7987200 | tf_op jit(solution)/shard_map/all_gather | solution.py:61
  22.0 432.2 %copy-start = (s32[96,3,640]{2,0,1:T(8,128)S(1)}, s32[96,3,640]{2,0,1:T(8,128)}, u32[]{:S(2)}) copy-start(s32[96,3,640]{2,0,1:T(8,128)} %param.14) | copy-start | bytes 2211844
  22.0 432.8 %copy-start.1 = (f32[640]{0:T(1024)S(1)}, f32[640]{0:T(1024)}, u32[]{:S(2)}) copy-start(f32[640]{0:T(1024)} %param.16) | copy-start | bytes 7684
  459.3 9.3 copy-start.2
  459.3 354.6 %all-to-all-start = ((bf16[64,96,640]{2,1,0:T(8,128)(2,1)}), bf16[64,96,640]{2,1,0:T(8,128)(2,1)}, u32[]{:S(2)}, u32[]{:S(2)}) async-start(bf16[64,96,640]{2,1,0:T(8,128)(2,1)} %stack.21), calls=%async_computation | async-start | bytes 15728640 | tf_op jit(solution)/shard_map/all_to_all | solution.py:63
  467.6 638.3 %all-gather.8.cloned.1.call-start = ((), (), s32[]{:S(2)}) async-start(), calls=%async_computation.4 | async-start | bytes 6656000 | tf_op jit(solution)/shard_map/all_gather | solution.py:92
  468.3 719.3 %reduce-scatter.4.cloned.1.call-start = ((), (), s32[]{:S(2)}) async-start(), calls=%async_computation.5 | async-start | bytes 1228800
Sparse Core Ops, SparseCore 0:
  9.2 436.6 all-gather.3
  455.7 358.1 all-gather.5
  815.7 290.1 all-gather.7
  1112.0 75.5 reduce-scatter.3
